TPU v7x, 32 devices: a whole 2x2x4 slice. The times are simulated.
32 devices in a mesh: groups: 2 (over y), row: 4 (over z), col: 4 (over x, core).
Axes of the slice: x: 2, y: 2, z: 4, core: 2. Of those that a mesh axis runs over, the one named last changes fastest.
Arguments:
- right_side: float32 [4096, 512], P(('groups', 'row')), parts along dimension 0, may hold values from -6 to 6
- prev_factor: float32 [4096, 4096], P(('groups', 'row'), 'col'), parts along dimension 0, may hold values from -0.09375 to 0.09375
- prev_solution: float32 [8192, 512], P(('groups', 'col'), 'row'), parts along dimension 0, may hold values from -6 to 6
- window_factor: float32 [4096, 1536], P(('groups', 'row')), parts along dimension 0, may hold values from -2 to 2
Outputs:
- panel: float32 [4096, 512], P(('groups', 'row'), 'col'), parts along dimension 0
There are 2 independent parts, one for each index of `groups`. A program takes and returns all parts, laid end to end along the dimension named above; each array names one. Nothing has to cross between parts.
All inputs are finite; a program needn't handle non-finite values.
Results may differ from a plain program's by a relative error of at most 0.0001.
Values sent between devices are 32-bit elements; how exact they have to be, the bound alone decides.
No kernel may reach another device: no remote copies, remote signals or barrier semaphores. Data moves between devices by JAX's collectives and lax.ppermute only.
A program may use at most 64 MiB of HBM per device.

v0:
```python
import jax
import jax.numpy as jnp
from jax import lax
from jax.sharding import PartitionSpec as P

NRHS = 512
STEPS = 6


def spread(array, axis, root):
    mine = lax.axis_index(axis) == root
    return lax.psum(jnp.where(mine, array, jnp.zeros_like(array)), axis)


def advance(resid, tiles, order, step, slot, is_root, sender):
    local = resid[slot]

    def solve_tile():
        return jnp.dot(
            tiles[slot, :, step, :],
            local,
            precision=lax.Precision.HIGHEST,
            preferred_element_type=jnp.float32,
        )

    def empty_tile():
        return jnp.zeros_like(local)

    mine = lax.cond(is_root, solve_tile, empty_tile)
    solved = sender(mine)
    update = jnp.einsum(
        "sij,jn->sin", tiles[:, :, step, :], solved, precision=lax.Precision.HIGHEST
    )
    later = (order > step)[:, None, None]
    resid = jnp.where(later, resid - update, resid)
    resid = jnp.where((order == step)[:, None, None], solved[None], resid)
    return resid


def body(right_side, prev_factor, prev_solution, window_factor):
    row_count = lax.axis_size("row")
    row_index = lax.axis_index("row")
    col_count = lax.axis_size("col")
    col_index = lax.axis_index("col")
    blocks = window_factor.shape[1] // STEPS
    slots = right_side.shape[0] // blocks
    partial_value = jnp.dot(
        prev_factor,
        lax.all_gather(prev_solution, "row", axis=1, tiled=True),
        precision=lax.Precision.HIGHEST,
        preferred_element_type=jnp.float32,
    )
    tiles = window_factor.reshape(slots, blocks, STEPS, blocks)
    order = jnp.arange(slots, dtype=jnp.int32) * row_count + row_index
    prior = lax.psum(partial_value, "col")
    resid = (right_side - prior).reshape(slots, blocks, -1)
    for step in range(STEPS):
        root = step % row_count
        resid = advance(
            resid,
            tiles,
            order,
            step,
            step // row_count,
            row_index == root,
            lambda solved: spread(solved, "row", root),
        )
    width = NRHS // col_count
    return lax.dynamic_slice_in_dim(resid.reshape(slots * blocks, -1), col_index * width, width, 1)


def solution(mesh):
    in_specs = (
        P(("groups", "row"), None),
        P(("groups", "row"), "col"),
        P(("groups", "col"), "row"),
        P(("groups", "row"), None),
    )
    out_specs = P(("groups", "row"), "col")
    return jax.shard_map(body, mesh=mesh, in_specs=in_specs, out_specs=out_specs, check_vma=False)
```

profile of v0, /device:TPU:0, one launch (start us, length us, event | category | flops | bytes accessed | tf_op | source)
XLA Modules:
  0.0 414.7 jit_solution(410126882840946337)
XLA Ops:
  7.3 50.6 %all-gather.2.cloned.1.call-done = f32[1024,512]{1,0:T(8,128)} async-done(((f32[1024,128]{1,0:T(8,128)}), f32[1024,512]{1,0:T(8,128)}) %all-gather.2.cloned.1.call-update) | async-done | bytes 2097168 | tf_op jit(solution)/shard_map/all_gather | solution.py:49
  57.9 6.1 %fusion.48 = f32[512,512]{1,0:T(8,128)} fusion(f32[512,1024]{1,0:T(8,128)S(1)} %copy-done, f32[1024,512]{1,0:T(8,128)} %all-gather.2.cloned.1.call-done), kind=kOutput, calls=%fused_computation.80 | convolution fusion | flops 3221225472 | bytes 5242880 | tf_op jit(solution)/shard_map/dot_general | solution.py:47
  64.1 3.5 copy.11
  67.6 3.8 reshape.56
  71.4 27.1 %all-reduce.8.cloned.1.call-done = f32[512,512]{1,0:T(8,128)} async-done(((f32[512,512]{1,0:T(8,128)}), f32[512,512]{1,0:T(8,128)}) %all-reduce.8.cloned.1.call-update) | async-done | bytes 1048592 | tf_op jit(solution)/shard_map/psum | solution.py:55
  98.5 2.8 sub.21
  101.3 8.1 %conditional.6 = (f32[256,512]{1,0:T(8,128)}) conditional(s32[]{:T(128)} %convert_element_type.15, () %tuple.46, (f32[2,256,6,256]{1,0,3,2:T(2,128)S(1)}, f32[512,512]{1,0:T(8,128)}) %tuple.47), branch_computations={%region_1.0_spmd, %region_2.0_spmd} | conditional | flops 402653184 | bytes 8126472 | solution.py:29
  101.3 3.9 copy.12
  105.2 1.8 slice.67
  107.0 2.5 fusion
  109.4 1.9 broadcast_select_fusion.5
  111.4 2.4 fusion.47
  113.8 2.1 copy.30
  115.8 31.5 %all-reduce.10.cloned.1.call-done = f32[256,512]{1,0:T(8,128)} async-done(((f32[256,512]{1,0:T(8,128)}), f32[256,512]{1,0:T(8,128)}) %all-reduce.10.cloned.1.call-update) | async-done | bytes 524304 | tf_op jit(solution)/shard_map/psum | solution.py:12
  147.4 3.7 fusion.34
  151.1 0.9 conditional.7
  151.1 0.9 broadcast.155
  152.0 0.8 broadcast_select_fusion.4
  152.9 2.0 copy.31
  155.0 43.6 %all-reduce.12.cloned.1.call-done = f32[256,512]{1,0:T(8,128)} async-done(((f32[256,512]{1,0:T(8,128)}), f32[256,512]{1,0:T(8,128)}) %all-reduce.12.cloned.1.call-update) | async-done | bytes 524304 | tf_op jit(solution)/shard_map/psum | solution.py:12
  198.6 3.7 fusion.33
  202.3 0.9 conditional.8
  202.3 0.9 broadcast.156
  203.2 0.8 broadcast_select_fusion.3
  204.1 2.0 copy.32
  206.2 44.4 %all-reduce.14.cloned.1.call-done = f32[256,512]{1,0:T(8,128)} async-done(((f32[256,512]{1,0:T(8,128)}), f32[256,512]{1,0:T(8,128)}) %all-reduce.14.cloned.1.call-update) | async-done | bytes 524304 | tf_op jit(solution)/shard_map/psum | solution.py:12
  250.5 3.7 fusion.32
  254.3 0.9 conditional.9
  254.3 0.9 broadcast.157
  255.1 0.8 broadcast_select_fusion.2
  256.1 2.0 copy.33
  258.1 44.7 %all-reduce.16.cloned.1.call-done = f32[256,512]{1,0:T(8,128)} async-done(((f32[256,512]{1,0:T(8,128)}), f32[256,512]{1,0:T(8,128)}) %all-reduce.16.cloned.1.call-update) | async-done | bytes 524304 | tf_op jit(solution)/shard_map/psum | solution.py:12
  302.8 3.7 fusion.31
  306.6 8.2 %conditional.10 = (f32[256,512]{1,0:T(8,128)}) conditional(s32[]{:T(128)} %convert_element_type.15, () %tuple.42, (f32[2,256,6,256]{1,0,3,2:T(2,128)S(1)}, f32[2,256,512]{2,1,0:T(8,128)}) %tuple.51), branch_computations={%region_13.14_spmd, %region_14.15_spmd} | conditional | flops 402653184 | bytes 8126472 | solution.py:29
  306.6 3.9 copy.20
  310.5 1.9 slice.71
  312.4 2.5 fusion.19
  314.8 1.9 broadcast_select_fusion.1
  316.8 2.0 copy.34
  318.8 34.5 %all-reduce.18.cloned.1.call-done = f32[256,512]{1,0:T(8,128)} async-done(((f32[256,512]{1,0:T(8,128)}), f32[256,512]{1,0:T(8,128)}) %all-reduce.18.cloned.1.call-update) | async-done | bytes 524304 | tf_op jit(solution)/shard_map/psum | solution.py:12
  353.3 3.7 fusion.30
  357.1 0.9 conditional.11
  357.1 0.9 broadcast.159
  357.9 0.8 broadcast_select_fusion
  358.8 2.3 copy.35
  361.1 43.5 %all-reduce.20.cloned.1.call-done = f32[256,512]{1,0:T(8,128)} async-done(((f32[256,512]{1,0:T(8,128)}), f32[256,512]{1,0:T(8,128)}) %all-reduce.20.cloned.1.call-update) | async-done | bytes 524304 | tf_op jit(solution)/shard_map/psum | solution.py:12
  404.7 2.5 fusion.29
  407.1 0.7 constant_dynamic-slice_fusion
  (28 shorter events, 1.2 us)
Async XLA Ops:
  6.5 51.4 %copy-start = (f32[512,1024]{1,0:T(8,128)S(1)}, f32[512,1024]{1,0:T(8,128)}, u32[]{:S(2)}) copy-start(f32[512,1024]{1,0:T(8,128)} %param.17) | copy-start | bytes 6291460
  6.5 51.4 %all-gather.2.cloned.1.call-start = ((), (), s32[]{:S(2)}) async-start(), calls=%async_computation | async-start | bytes 2621440 | tf_op jit(solution)/shard_map/all_gather | solution.py:49
  7.3 91.3 %all-reduce.8.cloned.1.call-start = ((), (), s32[]{:S(2)}) async-start(), calls=%async_computation.1 | async-start | bytes 2097152 | tf_op jit(solution)/shard_map/psum | solution.py:55
  64.0 83.4 %all-reduce.10.cloned.1.call-start = ((), (), s32[]{:S(2)}) async-start(), calls=%async_computation.2 | async-start | bytes 1048576 | tf_op jit(solution)/shard_map/psum | solution.py:12
  111.3 87.3 %all-reduce.12.cloned.1.call-start = ((), (), s32[]{:S(2)}) async-start(), calls=%async_computation.3 | async-start | bytes 1048576 | tf_op jit(solution)/shard_map/psum | solution.py:12
  152.9 97.7 %all-reduce.14.cloned.1.call-start = ((), (), s32[]{:S(2)}) async-start(), calls=%async_computation.4 | async-start | bytes 1048576 | tf_op jit(solution)/shard_map/psum | solution.py:12
  204.1 98.8 %all-reduce.16.cloned.1.call-start = ((), (), s32[]{:S(2)}) async-start(), calls=%async_computation.5 | async-start | bytes 1048576 | tf_op jit(solution)/shard_map/psum | solution.py:12
  256.0 97.3 %all-reduce.18.cloned.1.call-start = ((), (), s32[]{:S(2)}) async-start(), calls=%async_computation.6 | async-start | bytes 1048576 | tf_op jit(solution)/shard_map/psum | solution.py:12
  316.7 87.9 %all-reduce.20.cloned.1.call-start = ((), (), s32[]{:S(2)}) async-start(), calls=%async_computation.7 | async-start | bytes 1048576 | tf_op jit(solution)/shard_map/psum | solution.py:12
  357.9 46.7 %copy-start.2 = (f32[2,256,512]{2,1,0:T(8,128)S(1)}, f32[2,256,512]{2,1,0:T(8,128)}, u32[]{:S(2)}) copy-start(f32[2,256,512]{2,1,0:T(8,128)} %fusion.30) | copy-start | bytes 3145732
  357.9 49.9 %copy-start.1 = (f32[512,1024]{1,0:T(8,128)S(1)}, f32[512,1024]{1,0:T(8,128)}, u32[]{:S(2)}) copy-start(f32[512,1024]{1,0:T(8,128)} %param.17) | copy-start | bytes 6291460
Sparse Core Ops, SparseCore 0:
  8.9 48.9 all-gather.1
  64.1 34.3 all-reduce.7
  111.4 35.8 all-reduce.9
  153.0 45.5 all-reduce.11
  204.2 46.2 all-reduce.13
  256.1 46.6 all-reduce.15
  316.9 36.4 all-reduce.17
  358.9 45.6 all-reduce.19
where the time goes:
time: 416 us; the launch traced here: 415 us
  waiting for transfers between devices  321 us (77%)
  local copies, waits for them, and re-layouts  37.9 us (9%)
  matrix products  32.2 us (8%)
  between operations  13.5 us (3%)
  other arithmetic  9.93 us (2%)
    psum x6, waiting for transfers between devices, spread(): return lax.psum(jnp.where(mine, array, jnp.zeros_like(array)), axis)  242 us
    all_gather x1, waiting for transfers between devices, body(): lax.all_gather(prev_solution, 'row', axis=1, tiled=True)  50.6 us
    psum x1, waiting for transfers between devices, body(): prior = lax.psum(partial_value, 'col')  27.1 us
    dot_general x6, matrix products, advance(): jnp.einsum('sij,jn->sin', tiles[:, :, step, :], solved, precision=lax.Pre...  21.2 us
    unnamed x13, local copies, waits for them, and re-layouts  16.1 us
    another operation x6, local copies, waits for them, and re-layouts  11.3 us
  transfers between devices with their start and end apart: 8, of which 8 were waited for; matrix products, arithmetic and copies ran while one was open for 5% of the time, Pallas kernels for 0%

commit v1 on v0

--- a/solution.py
+++ b/solution.py
@@ -9,7 +9,7 @@
 
 def spread(array, axis, root):
     mine = lax.axis_index(axis) == root
-    return lax.psum(jnp.where(mine, array, jnp.zeros_like(array)), axis)
+    return jnp.sum(lax.all_gather(jnp.where(mine, array, jnp.zeros_like(array)), axis), axis=0)
 
 
 def advance(resid, tiles, order, step, slot, is_root, sender):

time: 416 us -> 471 us (1.13)
  waiting for transfers between devices: 321 us -> 361 us
  other arithmetic: 9.93 us -> 26 us
    all_gather x0 -> x6, waiting for transfers between devices: none -> 282 us  [spread(): lax.all_gather(jnp.where(mine, array, jnp.zeros_like(array)), axis)]
    psum x6 -> x0, waiting for transfers between devices: 242 us -> none  [spread(): return lax.psum(jnp.where(mine, array, jnp.zeros_like(array)), axis)]
    reduce_sum x0 -> x6, other arithmetic: none -> 16.1 us  [spread(): jnp.sum(lax.all_gather(jnp.where(mine, array, jnp.zeros_like(array)), axi...]
where the time goes in v1:
time: 471 us; the launch traced here: 470 us
  waiting for transfers between devices  361 us (77%)
  local copies, waits for them, and re-layouts  36.8 us (8%)
  matrix products  32.2 us (7%)
  other arithmetic  26 us (6%)
  between operations  13.6 us (3%)
    all_gather x6, waiting for transfers between devices, spread(): lax.all_gather(jnp.where(mine, array, jnp.zeros_like(array)), axis)  282 us
    all_gather x1, waiting for transfers between devices, body(): lax.all_gather(prev_solution, 'row', axis=1, tiled=True)  50.6 us
    psum x1, waiting for transfers between devices, body(): prior = lax.psum(partial_value, 'col')  27.1 us
    dot_general x6, matrix products, advance(): jnp.einsum('sij,jn->sin', tiles[:, :, step, :], solved, precision=lax.Pre...  21.2 us
    reduce_sum x6, other arithmetic, spread(): jnp.sum(lax.all_gather(jnp.where(mine, array, jnp.zeros_like(array)), axi...  16.1 us
    unnamed x13, local copies, waits for them, and re-layouts  15.9 us
    another operation x6, local copies, waits for them, and re-layouts  10.4 us
  transfers between devices with their start and end apart: 8, of which 8 were waited for; matrix products, arithmetic and copies ran while one was open for 5% of the time, Pallas kernels for 0%

profile of v1, /device:TPU:0, one launch (start us, length us, event | category | flops | bytes accessed | tf_op | source)
XLA Modules:
  0.0 469.6 jit_solution(1269660258135148004)
XLA Ops:
  7.3 50.6 %all-gather.14.cloned.1.call-done = f32[1024,512]{1,0:T(8,128)} async-done(((f32[1024,128]{1,0:T(8,128)}), f32[1024,512]{1,0:T(8,128)}) %all-gather.14.cloned.1.call-update) | async-done | bytes 2097168 | tf_op jit(solution)/shard_map/all_gather | solution.py:49
  57.9 6.1 %fusion.48 = f32[512,512]{1,0:T(8,128)} fusion(f32[512,1024]{1,0:T(8,128)S(1)} %copy-done, f32[1024,512]{1,0:T(8,128)} %all-gather.14.cloned.1.call-done), kind=kOutput, calls=%fused_computation.80 | convolution fusion | flops 3221225472 | bytes 5242880 | tf_op jit(solution)/shard_map/dot_general | solution.py:47
  64.1 3.5 copy.11
  67.6 3.8 reshape.56
  71.4 27.1 %all-reduce.2.cloned.1.call-done = f32[512,512]{1,0:T(8,128)} async-done(((f32[512,512]{1,0:T(8,128)}), f32[512,512]{1,0:T(8,128)}) %all-reduce.2.cloned.1.call-update) | async-done | bytes 1048592 | tf_op jit(solution)/shard_map/psum | solution.py:55
  98.5 2.8 sub.21
  101.3 8.1 %conditional.6 = (f32[256,512]{1,0:T(8,128)}) conditional(s32[]{:T(128)} %convert_element_type.15, () %tuple.46, (f32[2,256,6,256]{1,0,3,2:T(2,128)S(1)}, f32[512,512]{1,0:T(8,128)}) %tuple.47), branch_computations={%region_1.0_spmd, %region_2.0_spmd} | conditional | flops 402653184 | bytes 8126472 | solution.py:29
  101.3 3.9 copy.12
  105.2 1.8 slice.67
  107.0 2.5 fusion
  109.4 1.9 broadcast_select_fusion.5
  111.4 2.4 fusion.47
  113.8 2.0 copy.30
  115.8 39.2 %all-gather.16.cloned.1.call-done = f32[1024,512]{1,0:T(8,128)} async-done(((f32[256,512]{1,0:T(8,128)}), f32[1024,512]{1,0:T(8,128)}) %all-gather.16.cloned.1.call-update) | async-done | bytes 2097168 | tf_op jit(solution)/shard_map/all_gather | solution.py:12
  155.0 2.7 reduce_sum.54
  157.7 3.7 fusion.34
  161.4 0.8 conditional.7
  161.4 0.8 broadcast.155
  162.3 0.8 broadcast_select_fusion.4
  163.2 2.0 copy.31
  165.2 49.9 %all-gather.18.cloned.1.call-done = f32[1024,512]{1,0:T(8,128)} async-done(((f32[256,512]{1,0:T(8,128)}), f32[1024,512]{1,0:T(8,128)}) %all-gather.18.cloned.1.call-update) | async-done | bytes 2097168 | tf_op jit(solution)/shard_map/all_gather | solution.py:12
  215.1 2.7 reduce_sum.55
  217.8 3.7 fusion.33
  221.5 0.8 conditional.8
  221.5 0.8 broadcast.156
  223.3 2.0 copy.32
  225.3 51.0 %all-gather.20.cloned.1.call-done = f32[1024,512]{1,0:T(8,128)} async-done(((f32[256,512]{1,0:T(8,128)}), f32[1024,512]{1,0:T(8,128)}) %all-gather.20.cloned.1.call-update) | async-done | bytes 2097168 | tf_op jit(solution)/shard_map/all_gather | solution.py:12
  276.4 2.7 reduce_sum.56
  279.0 3.7 fusion.32
  282.8 0.8 conditional.9
  282.8 0.8 broadcast.157
  284.5 2.0 copy.33
  286.6 51.1 %all-gather.22.cloned.1.call-done = f32[1024,512]{1,0:T(8,128)} async-done(((f32[256,512]{1,0:T(8,128)}), f32[1024,512]{1,0:T(8,128)}) %all-gather.22.cloned.1.call-update) | async-done | bytes 2097168 | tf_op jit(solution)/shard_map/all_gather | solution.py:12
  337.7 2.7 reduce_sum.57
  340.4 3.7 fusion.31
  344.1 8.2 %conditional.10 = (f32[256,512]{1,0:T(8,128)}) conditional(s32[]{:T(128)} %convert_element_type.15, () %tuple.42, (f32[2,256,6,256]{1,0,3,2:T(2,128)S(1)}, f32[2,256,512]{2,1,0:T(8,128)}) %tuple.51), branch_computations={%region_13.14_spmd, %region_14.15_spmd} | conditional | flops 402653184 | bytes 8126472 | solution.py:29
  344.1 3.9 copy.20
  348.0 1.9 slice.71
  349.9 2.5 fusion.19
  352.3 1.9 broadcast_select_fusion.1
  354.3 2.0 copy.34
  356.3 42.1 %all-gather.24.cloned.1.call-done = f32[1024,512]{1,0:T(8,128)} async-done(((f32[256,512]{1,0:T(8,128)}), f32[1024,512]{1,0:T(8,128)}) %all-gather.24.cloned.1.call-update) | async-done | bytes 2097168 | tf_op jit(solution)/shard_map/all_gather | solution.py:12
  398.5 2.7 reduce_sum.58
  401.1 3.7 fusion.30
  405.8 2.1 copy.35
  407.9 48.8 %all-gather.26.cloned.1.call-done = f32[1024,512]{1,0:T(8,128)} async-done(((f32[256,512]{1,0:T(8,128)}), f32[1024,512]{1,0:T(8,128)}) %all-gather.26.cloned.1.call-update) | async-done | bytes 2097168 | tf_op jit(solution)/shard_map/all_gather | solution.py:12
  456.7 2.8 reduce_sum.59
  459.5 2.4 fusion.29
  (34 shorter events, 4.5 us)
Async XLA Ops:
  6.5 51.4 %copy-start = (f32[512,1024]{1,0:T(8,128)S(1)}, f32[512,1024]{1,0:T(8,128)}, u32[]{:S(2)}) copy-start(f32[512,1024]{1,0:T(8,128)} %param.17) | copy-start | bytes 6291460
  6.5 51.4 %all-gather.14.cloned.1.call-start = ((), (), s32[]{:S(2)}) async-start(), calls=%async_computation | async-start | bytes 2621440 | tf_op jit(solution)/shard_map/all_gather | solution.py:49
  7.3 91.3 %all-reduce.2.cloned.1.call-start = ((), (), s32[]{:S(2)}) async-start(), calls=%async_computation.1 | async-start | bytes 2097152 | tf_op jit(solution)/shard_map/psum | solution.py:55
  64.0 91.0 %all-gather.16.cloned.1.call-start = ((), (), s32[]{:S(2)}) async-start(), calls=%async_computation.2 | async-start | bytes 2621440 | tf_op jit(solution)/shard_map/all_gather | solution.py:12
  111.3 103.8 %all-gather.18.cloned.1.call-start = ((), (), s32[]{:S(2)}) async-start(), calls=%async_computation.3 | async-start | bytes 2621440 | tf_op jit(solution)/shard_map/all_gather | solution.py:12
  163.1 113.2 %all-gather.20.cloned.1.call-start = ((), (), s32[]{:S(2)}) async-start(), calls=%async_computation.4 | async-start | bytes 2621440 | tf_op jit(solution)/shard_map/all_gather | solution.py:12
  223.2 114.5 %all-gather.22.cloned.1.call-start = ((), (), s32[]{:S(2)}) async-start(), calls=%async_computation.5 | async-start | bytes 2621440 | tf_op jit(solution)/shard_map/all_gather | solution.py:12
  284.5 114.0 %all-gather.24.cloned.1.call-start = ((), (), s32[]{:S(2)}) async-start(), calls=%async_computation.6 | async-start | bytes 2621440 | tf_op jit(solution)/shard_map/all_gather | solution.py:12
  354.2 102.5 %all-gather.26.cloned.1.call-start = ((), (), s32[]{:S(2)}) async-start(), calls=%async_computation.7 | async-start | bytes 2621440 | tf_op jit(solution)/shard_map/all_gather | solution.py:12
  405.8 53.8 %copy-start.2 = (f32[2,256,512]{2,1,0:T(8,128)S(1)}, f32[2,256,512]{2,1,0:T(8,128)}, u32[]{:S(2)}) copy-start(f32[2,256,512]{2,1,0:T(8,128)} %fusion.30) | copy-start | bytes 3145732
  456.7 6.0 %copy-start.1 = (f32[512,1024]{1,0:T(8,128)S(1)}, f32[512,1024]{1,0:T(8,128)}, u32[]{:S(2)}) copy-start(f32[512,1024]{1,0:T(8,128)} %param.17) | copy-start | bytes 6291460
Sparse Core Ops, SparseCore 0:
  8.9 48.9 all-gather.13
  64.1 34.3 all-reduce.1
  111.4 43.5 all-gather.15
  163.3 51.8 all-gather.17
  223.4 52.9 all-gather.19
  284.6 53.0 all-gather.21
  354.4 44.0 all-gather.23
  405.9 50.7 all-gather.25
